TPU v7x, 256 devices: a whole 4x4x8 slice. The times are simulated.
256 devices in a mesh: seq: 64 (over z, y, core), batch: 4 (over x).
Axes of the slice: x: 4, y: 4, z: 8, core: 2. Of those that a mesh axis runs over, the one named last changes fastest.
Arguments:
- tokens: bfloat16 [32768, 1440], P(('batch', 'seq')), parts along dimension 0, may hold values from -6 to 6
- norm_gain: float32 [1440], replicated, may hold values from 0.1 to 1.9
- qkv_weight: bfloat16 [1440, 2560], P(None, 'seq'), may hold values from -2 to 2
- sinks: float32 [32], replicated, may hold values from 0 to 5
- out_weight: bfloat16 [2048, 1440], P('seq'), may hold values from -0.125 to 0.125
- moe_gain: float32 [1440], replicated, may hold values from 0.1 to 1.9
- expert_in: bfloat16 [64, 1440, 2880], P('seq'), may hold values from -0.15625 to 0.15625
- expert_out: bfloat16 [64, 1440, 1440], P('seq'), may hold values from -0.15625 to 0.15625
- expert_ids: int32 [32768, 4], P(('batch', 'seq')), parts along dimension 0, may hold values from 0 to 63, all different within a row; in each aligned block of 128 rows (0 to 127, 128 to 255, ...) at most 16 rows name the same one
- gate_ints: int32 [32768, 4], P(('batch', 'seq')), parts along dimension 0, may hold values from 1 to 4096
Outputs:
- block_out: bfloat16 [32768, 1440], P(('batch', 'seq')), parts along dimension 0
There are 4 independent parts, one for each index of `batch`. A program takes and returns all parts, laid end to end along the dimension named above; an argument that names none is the same for every part. Nothing has to cross between parts.
Inputs may be any that keep to these rules, and one draw needn't show every extreme that they name: `expert_ids`: each row names 4 different experts; among the 128 rows of one device no expert is named more than 16 times.
All inputs are finite; a program needn't handle non-finite values.
Results may differ from a plain program's by a relative error of at most 0.012.
Values may be sent and summed in bfloat16 or wider, within the bound.
No kernel may reach another device: no remote copies, remote signals or barrier semaphores. Data moves between devices by JAX's collectives and lax.ppermute only.
A program may use at most 128 MiB of HBM per device.

v0:
```python
import math

import jax
import jax.numpy as jnp
from jax import lax
from jax.sharding import PartitionSpec as P

QH = 32
KVH = 4
HD = 64
WIN = 128
TOP = 4


epsilon = 1e-05
rope_base = 150000.0
glu_slope = 1.702


def shifted(value, axis, steps):
    count = lax.axis_size(axis)
    initial, last = (max(0, -steps), min(count, count - steps))
    return lax.ppermute(value, axis, [(source, source + steps) for source in range(initial, last)])


def grouped_exchange(x, axis, split_dim, concat_dim, work, item_dim, out_dim):

    def moved(group):
        return lax.all_to_all(group, axis, split_axis=split_dim, concat_axis=concat_dim, tiled=True)

    items = jax.tree.leaves(x)[0].shape[item_dim]
    ends = [items * k // 2 for k in range(2 + 1)] if items % 2 == 0 else [0, items]
    groups = [
        jax.tree.map(lambda a: lax.slice_in_dim(a, low, high, axis=item_dim), x)
        for low, high in zip(ends, ends[1:])
    ]
    arrived = [moved(group) for group in groups]
    made = [work(group) for group in arrived]
    return jax.tree.map(lambda *parts: jnp.concatenate(parts, axis=out_dim), *made)


def norm_scale(values, gain):
    widened = values.astype(jnp.float32)
    mean_sq = jnp.mean(widened * widened, axis=-1, keepdims=True)
    return widened * lax.rsqrt(mean_sq + epsilon) * gain


def rotate(values, positions):
    half_width = values.shape[-1] // 2
    freq_steps = jnp.arange(half_width).astype(jnp.float32)
    inverse = jnp.exp(freq_steps * (-2.0 * math.log(rope_base) / values.shape[-1]))
    angles = positions[:, None] * inverse[None, :]
    cosine = jnp.cos(angles)[:, None, :]
    sine_term = jnp.sin(angles)[:, None, :]
    lower_half = values[..., :half_width]
    second = values[..., half_width:]
    return jnp.concatenate(
        [lower_half * cosine - second * sine_term, second * cosine + lower_half * sine_term],
        axis=-1,
    )


def band_block(queries, key_heads, value_heads, sinks, first_pos):
    count = queries.shape[0]
    groups = QH // KVH
    grouped = queries.reshape(count, KVH, groups, HD)
    scores = jnp.einsum(
        "tkgd,skd->kgts", grouped, key_heads, preferred_element_type=jnp.float32
    ) * (1.0 / math.sqrt(HD))
    query_pos = first_pos + jnp.arange(count)
    key_pos = first_pos - count + jnp.arange(2 * count)
    distance = query_pos[:, None] - key_pos[None, :]
    allowed = (distance >= 0) & (distance < WIN) & (key_pos >= 0)[None, :]
    scores = jnp.where(allowed[None, None, :, :], scores, -jnp.inf)
    sink_logit = sinks.reshape(KVH, groups, 1, 1)
    row_peak = jnp.maximum(jnp.max(scores, axis=-1, keepdims=True), sink_logit)
    raised = jnp.exp(scores - row_peak)
    totals = jnp.sum(raised, axis=-1, keepdims=True) + jnp.exp(sink_logit - row_peak)
    weights = (raised / totals).astype(jnp.bfloat16)
    mixture = jnp.einsum("kgts,skd->tkgd", weights, value_heads, preferred_element_type=jnp.float32)
    return mixture.reshape(count, QH * HD).astype(jnp.bfloat16)


def run_expert(incoming, weight_in, weight_out):
    width = incoming.shape[-1]
    hidden_width = weight_in.shape[1] // 2
    flat_rows = incoming.reshape(-1, width)
    paired = jnp.dot(flat_rows, weight_in, preferred_element_type=jnp.float32)
    gate_part = paired[:, :hidden_width]
    up_part = paired[:, hidden_width:]
    activated = (gate_part * jax.nn.sigmoid(glu_slope * gate_part) * (up_part + 1.0)).astype(
        jnp.bfloat16
    )
    produced = jnp.dot(activated, weight_out, preferred_element_type=jnp.float32).astype(
        jnp.bfloat16
    )
    return produced.reshape(incoming.shape)


def local(
    tokens,
    norm_gain,
    qkv_weight,
    sinks,
    out_weight,
    moe_gain,
    expert_in,
    expert_out,
    expert_ids,
    gate_ints,
):
    local_rows = tokens.shape[0]
    width = tokens.shape[1]
    devices = lax.axis_size("seq")
    device_index = lax.axis_index("seq")
    capacity = 2 * local_rows * TOP // devices
    query_cols = QH * HD
    key_cols = KVH * HD
    residual = tokens.astype(jnp.float32)
    normed = norm_scale(tokens, norm_gain).astype(jnp.bfloat16)
    projections = jnp.dot(
        normed,
        lax.all_gather(qkv_weight, "seq", axis=1, tiled=True),
        preferred_element_type=jnp.float32,
    )
    first_pos = device_index * local_rows
    positions = (first_pos + jnp.arange(local_rows)).astype(jnp.float32)
    queries = rotate(projections[:, :query_cols].reshape(local_rows, QH, HD), positions).astype(
        jnp.bfloat16
    )
    key_heads = rotate(
        projections[:, query_cols : query_cols + key_cols].reshape(local_rows, KVH, HD), positions
    ).astype(jnp.bfloat16)
    value_heads = (
        projections[:, query_cols + key_cols :].reshape(local_rows, KVH, HD).astype(jnp.bfloat16)
    )
    prev_keys, prev_values = shifted((key_heads, value_heads), "seq", 1)
    key_block = jnp.concatenate([prev_keys, key_heads], axis=0)
    value_block = jnp.concatenate([prev_values, value_heads], axis=0)
    attention = band_block(queries, key_block, value_block, sinks, first_pos)
    projected = jnp.dot(
        attention,
        lax.all_gather(out_weight, "seq", axis=0, tiled=True),
        preferred_element_type=jnp.float32,
    )
    residual_mid = (residual + projected).astype(jnp.bfloat16)
    moe_input = norm_scale(residual_mid, moe_gain).astype(jnp.bfloat16)
    flat_ids = expert_ids.reshape(-1)
    onehot = (flat_ids[:, None] == jnp.arange(devices)[None, :]).astype(jnp.int32)
    before = jnp.cumsum(onehot, axis=0) - onehot
    slot_index = jnp.sum(before * onehot, axis=1)
    target = flat_ids * capacity + slot_index
    matches = target[None, :] == jnp.arange(devices * capacity)[:, None]
    owner_row = jnp.sum(jnp.where(matches, jnp.arange(local_rows * TOP)[None, :], 0), axis=1)
    filled = jnp.any(matches, axis=1)
    gathered = jnp.take(moe_input, owner_row // TOP, axis=0)
    outgoing = jnp.where(filled[:, None], gathered, jnp.zeros_like(gathered)).reshape(
        devices, capacity, width
    )

    def serve_rows(incoming):
        return lax.all_to_all(
            run_expert(incoming, expert_in[0], expert_out[0]),
            "seq",
            split_axis=0,
            concat_axis=0,
            tiled=True,
        )

    returned = grouped_exchange(outgoing, "seq", 0, 0, serve_rows, 1, 1)
    picked = jnp.take(returned.reshape(-1, width), target, axis=0).reshape(local_rows, TOP, width)
    route_weight = gate_ints.astype(jnp.float32)
    route_weight = route_weight / jnp.sum(route_weight, axis=-1, keepdims=True)
    combined = residual_mid.astype(jnp.float32)
    for which in range(TOP):
        combined = combined + route_weight[:, which : which + 1] * picked[:, which].astype(
            jnp.float32
        )
    return combined.astype(jnp.bfloat16)


def solution(mesh):
    return jax.shard_map(
        local,
        mesh=mesh,
        in_specs=(
            P(("batch", "seq"), None),
            P(),
            P(None, "seq"),
            P(),
            P("seq", None),
            P(),
            P("seq", None, None),
            P("seq", None, None),
            P(("batch", "seq"), None),
            P(("batch", "seq"), None),
        ),
        out_specs=P(("batch", "seq"), None),
        check_vma=False,
    )
```

profile of v0, /device:TPU:1, one launch (start us, length us, event | category | flops | bytes accessed | tf_op | source)
XLA Modules:
  0.0 390.7 jit_solution(12637680279542303424)
XLA Ops:
  9.0 1.3 max.18
  10.3 1.2 reduce-window.6
  13.4 1.2 fusion.33
  15.5 81.1 %all-gather.3.cloned.1.call-done = bf16[1440,2560]{0,1:T(8,128)(2,1)} async-done(((bf16[1440,40]{0,1:T(8,128)(2,1)}), bf16[1440,2560]{0,1:T(8,128)(2,1)}) %all-gather.3.cloned.1.call-update) | async-done | bytes 7372816 | tf_op jit(solution)/shard_map/all_gather | solution.py:123
  96.6 6.4 %fusion.45 = f32[128,2560]{1,0:T(8,128)S(1)} fusion(bf16[1440,2560]{0,1:T(8,128)(2,1)} %all-gather.3.cloned.1.call-done, bf16[128,1440]{0,1:T(8,128)(2,1)} %param.10, f32[1440]{0:T(1024)} %param.11, f32[128]{0:T(128)S(1)} %add_rsqrt_fusion.1), kind=kOutput, calls=%fused_computation.62 | convolution fusion | flops 944455680 | bytes 9058432 | tf_op jit(solution)/shard_map/dot_general | solution.py:121
  103.9 2.0 collective-permute-start.1
  106.5 2.2 collective-permute-start
  108.7 1.6 fusion.9
  111.4 1.2 fusion.32
  112.6 64.1 %all-gather.5.cloned.1.call-done = bf16[2048,1440]{1,0:T(8,128)(2,1)} async-done(((bf16[32,1440]{1,0:T(8,128)(2,1)}), bf16[2048,1440]{1,0:T(8,128)(2,1)}) %all-gather.5.cloned.1.call-update) | async-done | bytes 5898256 | tf_op jit(solution)/shard_map/all_gather | solution.py:143
  176.7 5.0 %multiply_reduce_fusion = (f32[128]{0:T(128)S(1)}, f32[128,1440]{0,1:T(8,128)S(1)}) fusion(bf16[128,2048]{0,1:T(8,128)(2,1)S(1)} %bitcast.112, bf16[2048,1440]{1,0:T(8,128)(2,1)} %all-gather.5.cloned.1.call-done, bf16[128,1440]{0,1:T(8,128)(2,1)S(1)} %copy-done.3), kind=kOutput, calls=%fused_computation.55 | convolution fusion | flops 756080512 | bytes 7528960 | tf_op jit(solution)/shard_map/dot_general | solution.py:141
  183.0 4.6 %gather_fusion = bf16[1024,1440]{1,0:T(8,128)(2,1)S(1)} fusion(bf16[128,1440]{1,0:T(8,128)(2,1)S(1)} %copy.56, s32[1024]{0:T(1024)} %broadcast_clamp_fusion), kind=kCustom, calls=%fused_computation | custom fusion | bytes 5902336 | tf_op jit(solution)/shard_map/jit(_take)/gather | solution.py:156
  188.3 1.4 fusion.72
  189.6 44.5 %all_to_all.20 = bf16[64,8,1440]{2,1,0:T(8,128)(2,1)S(1)} all-to-all(bf16[64,8,1440]{2,1,0:T(8,128)(2,1)S(1)} %get-tuple-element.5), channel_id=1, replica_groups=mesh['seq'=64,'batch'=4] {'seq'}, dimensions={0} | all-to-all | bytes 2949120 | tf_op jit(solution)/shard_map/all_to_all | solution.py:29
  234.1 6.4 %all-to-all-start.2 = ((bf16[64,8,1440]{2,1,0:T(8,128)(2,1)}), bf16[64,8,1440]{2,1,0:T(8,128)(2,1)S(1)}, u32[]{:S(2)}, u32[]{:S(2)}) async-start(bf16[64,8,1440]{2,1,0:T(8,128)(2,1)} %get-tuple-element.6), calls=%async_computation.2 | async-start | bytes 3145728 | tf_op jit(solution)/shard_map/all_to_all | solution.py:29
  240.5 7.7 %fusion.2 = f32[512,2880]{0,1:T(8,128)S(1)} fusion(bf16[1,1440,2880]{2,1,0:T(8,128)(2,1)} %param.16, bf16[64,8,1440]{2,1,0:T(8,128)(2,1)S(1)} %all_to_all.20), kind=kOutput, calls=%fused_computation.4 | convolution fusion | flops 4246732800 | bytes 15667200 | tf_op jit(solution)/shard_map/dot_general | solution.py:88
  248.2 4.9 %fusion.10 = bf16[512,1440]{0,1:T(8,128)(2,1)S(1)} fusion(bf16[1,1440,1440]{2,1,0:T(8,128)(2,1)} %param.17, f32[512,2880]{0,1:T(8,128)S(1)} %fusion.2), kind=kOutput, calls=%fused_computation.17 | convolution fusion | flops 2130001920 | bytes 11520000 | tf_op jit(solution)/shard_map/dot_general | solution.py:94
  253.1 1.6 copy.57
  254.6 24.9 %all-to-all-done.2 = bf16[64,8,1440]{2,1,0:T(8,128)(2,1)S(1)} async-done(((bf16[64,8,1440]{2,1,0:T(8,128)(2,1)}), bf16[64,8,1440]{2,1,0:T(8,128)(2,1)S(1)}, u32[]{:S(2)}, u32[]{:S(2)}) %all-to-all-start.2) | async-done | bytes 1474592 | tf_op jit(solution)/shard_map/all_to_all | solution.py:29
  279.5 6.4 %all-to-all-start.1 = ((bf16[64,8,1440]{2,1,0:T(8,128)(2,1)}), bf16[64,8,1440]{2,1,0:T(8,128)(2,1)S(1)}, u32[]{:S(2)}, u32[]{:S(2)}) async-start(bf16[64,8,1440]{2,1,0:T(8,128)(2,1)} %bitcast.20), calls=%async_computation.1 | async-start | bytes 3145728 | tf_op jit(solution)/shard_map/all_to_all | solution.py:162
  285.9 7.7 %fusion = f32[512,2880]{0,1:T(8,128)S(1)} fusion(bf16[1,1440,2880]{2,1,0:T(8,128)(2,1)} %param.16, bf16[64,8,1440]{2,1,0:T(8,128)(2,1)S(1)} %all-to-all-done.2), kind=kOutput, calls=%fused_computation.2 | convolution fusion | flops 4246732800 | bytes 15667200 | tf_op jit(solution)/shard_map/dot_general | solution.py:88
  293.6 4.9 %fusion.13 = bf16[512,1440]{0,1:T(8,128)(2,1)S(1)} fusion(bf16[1,1440,1440]{2,1,0:T(8,128)(2,1)} %param.17, f32[512,2880]{0,1:T(8,128)S(1)} %fusion), kind=kOutput, calls=%fused_computation.18 | convolution fusion | flops 2130001920 | bytes 11520000 | tf_op jit(solution)/shard_map/dot_general | solution.py:94
  298.5 1.6 copy.58
  300.1 24.8 %all-to-all-done.1 = bf16[64,8,1440]{2,1,0:T(8,128)(2,1)S(1)} async-done(((bf16[64,8,1440]{2,1,0:T(8,128)(2,1)}), bf16[64,8,1440]{2,1,0:T(8,128)(2,1)S(1)}, u32[]{:S(2)}, u32[]{:S(2)}) %all-to-all-start.1) | async-done | bytes 1474592 | tf_op jit(solution)/shard_map/all_to_all | solution.py:162
  325.0 6.5 %all-to-all-start.3 = ((bf16[64,8,1440]{2,1,0:T(8,128)(2,1)}), bf16[64,8,1440]{2,1,0:T(8,128)(2,1)}, u32[]{:S(2)}, u32[]{:S(2)}) async-start(bf16[64,8,1440]{2,1,0:T(8,128)(2,1)} %bitcast.22), calls=%async_computation.3 | async-start | bytes 3145728 | tf_op jit(solution)/shard_map/all_to_all | solution.py:162
  332.1 38.5 %all-to-all-done.3 = bf16[64,8,1440]{2,1,0:T(8,128)(2,1)} async-done(((bf16[64,8,1440]{2,1,0:T(8,128)(2,1)}), bf16[64,8,1440]{2,1,0:T(8,128)(2,1)}, u32[]{:S(2)}, u32[]{:S(2)}) %all-to-all-start.3) | async-done | bytes 1474592 | tf_op jit(solution)/shard_map/all_to_all | solution.py:162
  370.5 2.4 pad_maximum_fusion
  372.9 3.0 gather_fusion.1
  375.9 2.9 gather.15
  378.8 2.4 copy.60
  381.2 1.5 broadcast_select_fusion
  382.8 1.1 fusion.37
  (77 shorter events, 10.0 us)
Async XLA Ops:
  6.5 90.1 %all-gather.3.cloned.1.call-start = ((), (), s32[]{:S(2)}) async-start(), calls=%async_computation.4 | async-start | bytes 7987200 | tf_op jit(solution)/shard_map/all_gather | solution.py:123
  7.3 169.4 %all-gather.5.cloned.1.call-start = ((), (), s32[]{:S(2)}) async-start(), calls=%async_computation.5 | async-start | bytes 6389760 | tf_op jit(solution)/shard_map/all_gather | solution.py:143
  12.0 0.6 copy-start.4
  103.9 4.8 %collective-permute-start.1 = (bf16[128,4,64]{0,2,1:T(8,128)(2,1)}, bf16[128,4,64]{0,2,1:T(8,128)(2,1)}, u32[]{:S(2)}, u32[]{:S(2)}) collective-permute-start(bf16[128,4,64]{0,2,1:T(8,128)(2,1)} %pad_maximum_fusion.1), channel_id=1, source_target_pairs={{0,4},{4,8},{8,12},{12,16},{16,20},{20,24},{24,28},{28,32},{32,36}... | collective-permute-start | bytes 196616 | tf_op jit(solution)/shard_map/ppermute | solution.py:23
  106.3 3.9 %copy-start.6 = (f32[4,8]{1,0:T(4,128)S(1)}, f32[4,8]{1,0:T(4,128)}, u32[]{:S(2)}) copy-start(f32[4,8]{1,0:T(4,128)} %max.18) | copy-start | bytes 388
  106.5 4.9 %collective-permute-start = (bf16[128,4,64]{0,2,1:T(8,128)(2,1)S(1)}, bf16[128,4,64]{0,2,1:T(8,128)(2,1)S(1)}, u32[]{:S(2)}, u32[]{:S(2)}) collective-permute-start(bf16[128,4,64]{0,2,1:T(8,128)(2,1)S(1)} %bitcast.116), channel_id=1, source_target_pairs={{0,4},{4,8},{8,12},{12,16},{16,20},{20,24},{24,28},{28,32},{32,36}... | collective-permute-start | bytes 196616 | tf_op jit(solution)/shard_map/ppermute | solution.py:23
  111.4 65.3 %copy-start.3 = (bf16[128,1440]{0,1:T(8,128)(2,1)S(1)}, bf16[128,1440]{0,1:T(8,128)(2,1)}, u32[]{:S(2)}) copy-start(bf16[128,1440]{0,1:T(8,128)(2,1)} %param.10) | copy-start | bytes 1105924
  176.7 5.9 %copy-start.8 = (f32[1440]{0:T(1024)S(1)}, f32[1440]{0:T(1024)}, u32[]{:S(2)}) copy-start(f32[1440]{0:T(1024)} %param.15) | copy-start | bytes 17284
  181.7 0.9 copy-start
  234.1 45.4 %all-to-all-start.2 = ((bf16[64,8,1440]{2,1,0:T(8,128)(2,1)}), bf16[64,8,1440]{2,1,0:T(8,128)(2,1)S(1)}, u32[]{:S(2)}, u32[]{:S(2)}) async-start(bf16[64,8,1440]{2,1,0:T(8,128)(2,1)} %get-tuple-element.6), calls=%async_computation.2 | async-start | bytes 3145728 | tf_op jit(solution)/shard_map/all_to_all | solution.py:29
  279.5 45.4 %all-to-all-start.1 = ((bf16[64,8,1440]{2,1,0:T(8,128)(2,1)}), bf16[64,8,1440]{2,1,0:T(8,128)(2,1)S(1)}, u32[]{:S(2)}, u32[]{:S(2)}) async-start(bf16[64,8,1440]{2,1,0:T(8,128)(2,1)} %bitcast.20), calls=%async_computation.1 | async-start | bytes 3145728 | tf_op jit(solution)/shard_map/all_to_all | solution.py:162
  298.5 33.0 %copy-start.5 = (s32[512]{0:T(512)S(1)}, s32[512]{0:T(512)}, u32[]{:S(2)}) copy-start(s32[512]{0:T(512)} %copy-done.4) | copy-start | bytes 6148
  298.5 33.1 %copy-start.7 = (s32[128,4]{0,1:T(4,128)S(1)}, s32[128,4]{0,1:T(4,128)}, u32[]{:S(2)}) copy-start(s32[128,4]{0,1:T(4,128)} %param.18) | copy-start | bytes 6148
  298.5 33.4 %copy-start.9 = (s32[128,4]{0,1:T(4,128)S(1)}, s32[128,4]{0,1:T(4,128)}, u32[]{:S(2)}) copy-start(s32[128,4]{0,1:T(4,128)} %param.19) | copy-start | bytes 6148
  325.0 7.1 %copy-start.2 = (bf16[64,8,1440]{2,1,0:T(8,128)(2,1)}, bf16[64,8,1440]{2,1,0:T(8,128)(2,1)S(1)}, u32[]{:S(2)}) copy-start(bf16[64,8,1440]{2,1,0:T(8,128)(2,1)S(1)} %all-to-all-done.1) | copy-start | bytes 4423684
  325.0 45.5 %all-to-all-start.3 = ((bf16[64,8,1440]{2,1,0:T(8,128)(2,1)}), bf16[64,8,1440]{2,1,0:T(8,128)(2,1)}, u32[]{:S(2)}, u32[]{:S(2)}) async-start(bf16[64,8,1440]{2,1,0:T(8,128)(2,1)} %bitcast.22), calls=%async_computation.3 | async-start | bytes 3145728 | tf_op jit(solution)/shard_map/all_to_all | solution.py:162
  378.8 4.0 %copy-start.1 = (f32[128,1440]{0,1:T(8,128)S(1)}, f32[128,1440]{0,1:T(8,128)}, u32[]{:S(2)}) copy-start(f32[128,1440]{0,1:T(8,128)} %copy-done) | copy-start | bytes 2211844
Sparse Core Ops, SparseCore 0:
  10.1 86.4 all-gather.2
  99.3 77.2 all-gather.4
where the time goes:
time: 392 us; the launch traced here: 391 us
  waiting for transfers between devices  235 us (60%)
  blocking collectives  44.5 us (11%)
  matrix products  39.3 us (10%)
  starting transfers between devices  23.5 us (6%)
  local copies, waits for them, and re-layouts  22.8 us (6%)
  between operations  13.9 us (4%)
  other arithmetic  11.9 us (3%)
    all_gather x1, waiting for transfers between devices, local(): lax.all_gather(qkv_weight, 'seq', axis=1, tiled=True)  81.1 us
    all_gather x1, waiting for transfers between devices, local(): lax.all_gather(out_weight, 'seq', axis=0, tiled=True)  64.1 us
    all_to_all x2, waiting for transfers between devices, serve_rows(): lax.all_to_all(run_expert(incoming, expert_in[0], expert_out[0]), 'seq',...  63.3 us
    all_to_all x1, blocking collectives, moved(): lax.all_to_all(group, axis, split_axis=split_dim, concat_axis=concat_dim,...  44.5 us
    all_to_all x1, waiting for transfers between devices, moved(): lax.all_to_all(group, axis, split_axis=split_dim, concat_axis=concat_dim,...  24.9 us
    dot_general x2, matrix products, run_expert(): paired = jnp.dot(flat_rows, weight_in, preferred_element_type=jnp.float32)  15.3 us
    all_to_all x2, starting transfers between devices, serve_rows(): lax.all_to_all(run_expert(incoming, expert_in[0], expert_out[0]), 'seq',...  12.9 us
    dot_general x2, matrix products, run_expert(): jnp.dot(activated, weight_out, preferred_element_type=jnp.float32)  9.81 us
  transfers between devices with their start and end apart: 7, of which 5 were waited for; matrix products, arithmetic and copies ran while one was open for 12% of the time, Pallas kernels for 0%

commit v1 on v0

--- a/solution.py
+++ b/solution.py
@@ -21,22 +21,6 @@
     count = lax.axis_size(axis)
     initial, last = (max(0, -steps), min(count, count - steps))
     return lax.ppermute(value, axis, [(source, source + steps) for source in range(initial, last)])
-
-
-def grouped_exchange(x, axis, split_dim, concat_dim, work, item_dim, out_dim):
-
-    def moved(group):
-        return lax.all_to_all(group, axis, split_axis=split_dim, concat_axis=concat_dim, tiled=True)
-
-    items = jax.tree.leaves(x)[0].shape[item_dim]
-    ends = [items * k // 2 for k in range(2 + 1)] if items % 2 == 0 else [0, items]
-    groups = [
-        jax.tree.map(lambda a: lax.slice_in_dim(a, low, high, axis=item_dim), x)
-        for low, high in zip(ends, ends[1:])
-    ]
-    arrived = [moved(group) for group in groups]
-    made = [work(group) for group in arrived]
-    return jax.tree.map(lambda *parts: jnp.concatenate(parts, axis=out_dim), *made)
 
 
 def norm_scale(values, gain):
@@ -97,6 +81,15 @@
     return produced.reshape(incoming.shape)
 
 
+def route_slots(expert_ids, devices, capacity):
+    rows = expert_ids.shape[0]
+    flat_ids = expert_ids.reshape(-1)
+    onehot = (flat_ids[:, None] == jnp.arange(devices)[None, :]).astype(jnp.int32)
+    before = jnp.cumsum(onehot, axis=0) - onehot
+    slot_index = jnp.sum(before * onehot, axis=1)
+    return (flat_ids * capacity + slot_index).reshape(rows, TOP)
+
+
 def local(
     tokens,
     norm_gain,
@@ -116,11 +109,16 @@
     capacity = 2 * local_rows * TOP // devices
     query_cols = QH * HD
     key_cols = KVH * HD
+    qkv_part = qkv_weight.shape[1]
+
     residual = tokens.astype(jnp.float32)
     normed = norm_scale(tokens, norm_gain).astype(jnp.bfloat16)
-    projections = jnp.dot(
+    both = jnp.concatenate([qkv_weight.T, out_weight], axis=0)
+    gathered = lax.all_gather(both, "seq", axis=0)
+    projections = lax.dot_general(
         normed,
-        lax.all_gather(qkv_weight, "seq", axis=1, tiled=True),
+        gathered[:, :qkv_part].reshape(-1, width),
+        (((1,), (1,)), ((), ())),
         preferred_element_type=jnp.float32,
     )
     first_pos = device_index * local_rows
@@ -140,41 +138,50 @@
     attention = band_block(queries, key_block, value_block, sinks, first_pos)
     projected = jnp.dot(
         attention,
-        lax.all_gather(out_weight, "seq", axis=0, tiled=True),
+        gathered[:, qkv_part:].reshape(-1, width),
         preferred_element_type=jnp.float32,
     )
     residual_mid = (residual + projected).astype(jnp.bfloat16)
     moe_input = norm_scale(residual_mid, moe_gain).astype(jnp.bfloat16)
-    flat_ids = expert_ids.reshape(-1)
-    onehot = (flat_ids[:, None] == jnp.arange(devices)[None, :]).astype(jnp.int32)
-    before = jnp.cumsum(onehot, axis=0) - onehot
-    slot_index = jnp.sum(before * onehot, axis=1)
-    target = flat_ids * capacity + slot_index
-    matches = target[None, :] == jnp.arange(devices * capacity)[:, None]
-    owner_row = jnp.sum(jnp.where(matches, jnp.arange(local_rows * TOP)[None, :], 0), axis=1)
-    filled = jnp.any(matches, axis=1)
-    gathered = jnp.take(moe_input, owner_row // TOP, axis=0)
-    outgoing = jnp.where(filled[:, None], gathered, jnp.zeros_like(gathered)).reshape(
-        devices, capacity, width
-    )
-
-    def serve_rows(incoming):
-        return lax.all_to_all(
-            run_expert(incoming, expert_in[0], expert_out[0]),
-            "seq",
-            split_axis=0,
-            concat_axis=0,
-            tiled=True,
-        )
-
-    returned = grouped_exchange(outgoing, "seq", 0, 0, serve_rows, 1, 1)
-    picked = jnp.take(returned.reshape(-1, width), target, axis=0).reshape(local_rows, TOP, width)
+
+    target = route_slots(expert_ids, devices, capacity)
     route_weight = gate_ints.astype(jnp.float32)
     route_weight = route_weight / jnp.sum(route_weight, axis=-1, keepdims=True)
+    halves = 2
+    slots = devices * capacity // halves
+    depth = capacity // halves
+
+    def places_of(half):
+        row = jnp.arange(slots)
+        return row // depth * capacity + half * depth + row % depth
+
     combined = residual_mid.astype(jnp.float32)
-    for which in range(TOP):
-        combined = combined + route_weight[:, which : which + 1] * picked[:, which].astype(
-            jnp.float32
+    arrived = []
+    for half in range(halves):
+        places = places_of(half)
+        pick = sum(
+            (target[:, which][None, :] == places[:, None]).astype(jnp.bfloat16)
+            for which in range(TOP)
+        )
+        rows = jnp.dot(pick, moe_input, preferred_element_type=jnp.float32).astype(jnp.bfloat16)
+        rows = rows.reshape(devices, depth, width)
+        arrived.append(lax.all_to_all(rows, "seq", split_axis=0, concat_axis=0, tiled=True))
+    for half in range(halves):
+        made = run_expert(arrived[half], expert_in[0], expert_out[0])
+        back = lax.all_to_all(made, "seq", split_axis=0, concat_axis=0, tiled=True)
+        places = places_of(half)
+        share = sum(
+            jnp.where(
+                target[:, which][:, None] == places[None, :], route_weight[:, which : which + 1], 0.0
+            )
+            for which in range(TOP)
+        )
+        coarse = share.astype(jnp.bfloat16)
+        fine = (share - coarse.astype(jnp.float32)).astype(jnp.bfloat16)
+        flat = back.reshape(slots, width)
+        combined = combined + (
+            jnp.dot(coarse, flat, preferred_element_type=jnp.float32)
+            + jnp.dot(fine, flat, preferred_element_type=jnp.float32)
         )
     return combined.astype(jnp.bfloat16)
 

time: 392 us -> 336 us (0.86)
  blocking collectives: 44.5 us -> 0 us
  waiting for transfers between devices: 235 us -> 213 us
  starting transfers between devices: 23.5 us -> 32.4 us
  matrix products: 39.3 us -> 44.3 us
  other arithmetic: 11.9 us -> 7.7 us
    all_gather x2 -> x1, waiting for transfers between devices: 145 us -> 93.3 us  [local(): gathered = lax.all_gather(both, 'seq', axis=0)]
    all_to_all x1 -> x0, blocking collectives: 44.5 us -> none  [moved(): lax.all_to_all(group, axis, split_axis=split_dim, concat_axis=concat_dim,...]
    all_to_all x3 -> x4, waiting for transfers between devices: 88.2 us -> 119 us  [the longest x2 60.3 us: local(): back = lax.all_to_all(made, 'seq', split_axis=0, concat_axis=0, tiled=True)]
    gather x4 -> x0, local copies, waits for them, and re-layouts: 13 us -> none  [the longest x3 8.31 us: local(): jnp.take(returned.reshape(-1, width), target, axis=0)]
    all_to_all x3 -> x4, starting transfers between devices: 19.3 us -> 28.3 us  [the longest x2 15.3 us: local(): lax.all_to_all(rows, 'seq', split_axis=0, concat_axis=0, tiled=True)]
    slice x2 -> x3, local copies, waits for them, and re-layouts: 1.59 us -> 10.1 us  [the longest x1 6.12 us: local(): gathered[:, qkv_part:].reshape(-1, width)]
    dot_general x2 -> x8, matrix products: 11.4 us -> 14 us  [the longest x2 4.03 us: local(): jnp.dot(fine, flat, preferred_element_type=jnp.float32)]
  transfers between devices with their start and end apart: 7 -> 7, of which waited for: 5 -> 5; matrix products, arithmetic and copies ran while one was open for 12% -> 16% of each run, Pallas kernels for 0% -> 0%
where the time goes in v1:
time: 336 us; the launch traced here: 335 us
  waiting for transfers between devices  213 us (63%)
  matrix products  44.3 us (13%)
  starting transfers between devices  32.4 us (10%)
  local copies, waits for them, and re-layouts  24.8 us (7%)
  between operations  13.7 us (4%)
  other arithmetic  7.7 us (2%)
    all_gather x1, waiting for transfers between devices, local(): gathered = lax.all_gather(both, 'seq', axis=0)  93.3 us
    all_to_all x2, waiting for transfers between devices, local(): back = lax.all_to_all(made, 'seq', split_axis=0, concat_axis=0, tiled=True)  60.3 us
    all_to_all x2, waiting for transfers between devices, local(): lax.all_to_all(rows, 'seq', split_axis=0, concat_axis=0, tiled=True)  59 us
    dot_general x2, matrix products, run_expert(): paired = jnp.dot(flat_rows, weight_in, preferred_element_type=jnp.float32)  16.3 us
    all_to_all x2, starting transfers between devices, local(): lax.all_to_all(rows, 'seq', split_axis=0, concat_axis=0, tiled=True)  15.3 us
    all_to_all x2, starting transfers between devices, local(): back = lax.all_to_all(made, 'seq', split_axis=0, concat_axis=0, tiled=True)  12.9 us
    dot_general x2, matrix products, run_expert(): jnp.dot(activated, weight_out, preferred_element_type=jnp.float32)  12.1 us
  transfers between devices with their start and end apart: 7, of which 5 were waited for; matrix products, arithmetic and copies ran while one was open for 16% of the time, Pallas kernels for 0%

profile of v1, /device:TPU:1, one launch (start us, length us, event | category | flops | bytes accessed | tf_op | source)
XLA Modules:
  0.0 335.4 jit_solution(1335957733252972977)
XLA Ops:
  6.5 1.7 pad_maximum_fusion
  10.0 1.2 reduce-window.6
  11.9 1.2 fusion.41
  14.0 93.3 %all-gather.3.cloned.1.call-done = bf16[4608,1440]{1,0:T(8,128)(2,1)} async-done(((bf16[72,1440]{1,0:T(8,128)(2,1)}), bf16[4608,1440]{1,0:T(8,128)(2,1)}) %all-gather.3.cloned.1.call-update) | async-done | bytes 13271056 | tf_op jit(solution)/shard_map/all_gather | solution.py:117
  107.3 3.8 %slice.109 = bf16[64,40,1440]{2,1,0:T(8,128)(2,1)S(1)} slice(bf16[64,72,1440]{2,1,0:T(8,128)(2,1)} %bitcast.111), slice={[0:64], [0:40], [0:1440]} | slice | bytes 14745600 | tf_op jit(solution)/shard_map/slice | solution.py:120
  111.1 3.1 fusion.48
  114.5 2.0 collective-permute-start.1
  116.5 1.3 copy.48
  117.8 1.3 subtract_convert_fusion
  119.2 6.1 %slice.117 = bf16[64,32,1440]{2,1,0:T(8,128)(2,1)} slice(bf16[64,72,1440]{2,1,0:T(8,128)(2,1)} %bitcast.112), slice={[0:64], [40:72], [0:1440]} | slice | bytes 11796480 | tf_op jit(solution)/shard_map/slice | solution.py:141
  125.4 2.2 collective-permute-start
  129.4 1.2 fusion.40
  132.2 2.2 multiply_reduce_fusion
  135.1 1.6 copy.54
  136.7 8.9 %all-to-all-start = ((bf16[64,8,1440]{2,1,0:T(8,128)(2,1)}), bf16[64,8,1440]{2,1,0:T(8,128)(2,1)}, u32[]{:S(2)}, u32[]{:S(2)}) async-start(bf16[64,8,1440]{2,1,0:T(8,128)(2,1)} %bitcast.25), calls=%async_computation | async-start | bytes 3145728 | tf_op jit(solution)/shard_map/all_to_all | solution.py:168
  146.3 1.6 copy.56
  147.9 36.7 %all-to-all-done = bf16[64,8,1440]{2,1,0:T(8,128)(2,1)} async-done(((bf16[64,8,1440]{2,1,0:T(8,128)(2,1)}), bf16[64,8,1440]{2,1,0:T(8,128)(2,1)}, u32[]{:S(2)}, u32[]{:S(2)}) %all-to-all-start) | async-done | bytes 1474592 | tf_op jit(solution)/shard_map/all_to_all | solution.py:168
  184.6 6.4 %all-to-all-start.2 = ((bf16[64,8,1440]{2,1,0:T(8,128)(2,1)}), bf16[64,8,1440]{2,1,0:T(8,128)(2,1)S(1)}, u32[]{:S(2)}, u32[]{:S(2)}) async-start(bf16[64,8,1440]{2,1,0:T(8,128)(2,1)} %bitcast.31), calls=%async_computation.2 | async-start | bytes 3145728 | tf_op jit(solution)/shard_map/all_to_all | solution.py:168
  191.0 8.2 %fusion.2 = f32[512,2880]{0,1:T(8,128)S(1)} fusion(bf16[1,1440,2880]{2,1,0:T(8,128)(2,1)} %param.16, bf16[64,8,1440]{2,1,0:T(8,128)(2,1)} %all-to-all-done), kind=kOutput, calls=%fused_computation.2 | convolution fusion | flops 4246732800 | bytes 15667200 | tf_op jit(solution)/shard_map/dot_general | solution.py:72
  199.2 6.0 %fusion.10 = bf16[512,1440]{0,1:T(8,128)(2,1)} fusion(bf16[1,1440,1440]{2,1,0:T(8,128)(2,1)} %param.17, f32[512,2880]{0,1:T(8,128)S(1)} %fusion.2), kind=kOutput, calls=%fused_computation.13 | convolution fusion | flops 2130001920 | bytes 11520000 | tf_op jit(solution)/shard_map/dot_general | solution.py:78
  205.2 2.6 copy.55
  207.8 22.3 %all-to-all-done.2 = bf16[64,8,1440]{2,1,0:T(8,128)(2,1)S(1)} async-done(((bf16[64,8,1440]{2,1,0:T(8,128)(2,1)}), bf16[64,8,1440]{2,1,0:T(8,128)(2,1)S(1)}, u32[]{:S(2)}, u32[]{:S(2)}) %all-to-all-start.2) | async-done | bytes 1474592 | tf_op jit(solution)/shard_map/all_to_all | solution.py:168
  231.2 6.4 %all-to-all-start.1 = ((bf16[64,8,1440]{2,1,0:T(8,128)(2,1)}), bf16[64,8,1440]{2,1,0:T(8,128)(2,1)S(1)}, u32[]{:S(2)}, u32[]{:S(2)}) async-start(bf16[64,8,1440]{2,1,0:T(8,128)(2,1)} %bitcast.114), calls=%async_computation.1 | async-start | bytes 3145728 | tf_op jit(solution)/shard_map/all_to_all | solution.py:171
  237.6 8.2 %fusion = f32[512,2880]{0,1:T(8,128)S(1)} fusion(bf16[1,1440,2880]{2,1,0:T(8,128)(2,1)} %param.16, bf16[64,8,1440]{2,1,0:T(8,128)(2,1)} %copy-done.1), kind=kOutput, calls=%fused_computation | convolution fusion | flops 4246732800 | bytes 15667200 | tf_op jit(solution)/shard_map/dot_general | solution.py:72
  245.8 6.0 %fusion.13 = bf16[512,1440]{0,1:T(8,128)(2,1)} fusion(bf16[1,1440,1440]{2,1,0:T(8,128)(2,1)} %param.17, f32[512,2880]{0,1:T(8,128)S(1)} %fusion), kind=kOutput, calls=%fused_computation.14 | convolution fusion | flops 2130001920 | bytes 11520000 | tf_op jit(solution)/shard_map/dot_general | solution.py:78
  251.8 2.6 copy.57
  254.4 22.3 %all-to-all-done.1 = bf16[64,8,1440]{2,1,0:T(8,128)(2,1)S(1)} async-done(((bf16[64,8,1440]{2,1,0:T(8,128)(2,1)}), bf16[64,8,1440]{2,1,0:T(8,128)(2,1)S(1)}, u32[]{:S(2)}, u32[]{:S(2)}) %all-to-all-start.1) | async-done | bytes 1474592 | tf_op jit(solution)/shard_map/all_to_all | solution.py:171
  276.7 6.5 %all-to-all-start.3 = ((bf16[64,8,1440]{2,1,0:T(8,128)(2,1)}), bf16[64,8,1440]{2,1,0:T(8,128)(2,1)}, u32[]{:S(2)}, u32[]{:S(2)}) async-start(bf16[64,8,1440]{2,1,0:T(8,128)(2,1)} %bitcast.113), calls=%async_computation.3 | async-start | bytes 3145728 | tf_op jit(solution)/shard_map/all_to_all | solution.py:171
  284.2 38.0 %all-to-all-done.3 = bf16[64,8,1440]{2,1,0:T(8,128)(2,1)} async-done(((bf16[64,8,1440]{2,1,0:T(8,128)(2,1)}), bf16[64,8,1440]{2,1,0:T(8,128)(2,1)}, u32[]{:S(2)}, u32[]{:S(2)}) %all-to-all-start.3) | async-done | bytes 1474592 | tf_op jit(solution)/shard_map/all_to_all | solution.py:171
  322.2 2.3 fusion.27
  324.6 2.3 convolution_add_fusion
  326.9 1.7 fusion.22
  (60 shorter events, 10.6 us)
Async XLA Ops:
  6.5 100.8 %all-gather.3.cloned.1.call-start = ((), (), s32[]{:S(2)}) async-start(), calls=%async_computation.4 | async-start | bytes 14376960 | tf_op jit(solution)/shard_map/all_gather | solution.py:117
  107.3 3.8 %copy-start = (bf16[128,1440]{0,1:T(8,128)(2,1)S(1)}, bf16[128,1440]{0,1:T(8,128)(2,1)}, u32[]{:S(2)}) copy-start(bf16[128,1440]{0,1:T(8,128)(2,1)} %param.10) | copy-start | bytes 1105924
  107.3 3.8 %copy-start.3 = (f32[1440]{0:T(1024)S(1)}, f32[1440]{0:T(1024)}, u32[]{:S(2)}) copy-start(f32[1440]{0:T(1024)} %param.11) | copy-start | bytes 17284
  114.5 13.1 %collective-permute-start.1 = (bf16[128,4,64]{0,2,1:T(8,128)(2,1)S(1)}, bf16[128,4,64]{0,2,1:T(8,128)(2,1)S(1)}, u32[]{:S(2)}, u32[]{:S(2)}) collective-permute-start(bf16[128,4,64]{0,2,1:T(8,128)(2,1)S(1)} %pad_maximum_fusion.1), channel_id=1, source_target_pairs={{0,4},{4,8},{8,12},{12,16},{16,20},{20,24},{24,28},{28,32},{32,36}... | collective-permute-start | bytes 196616 | tf_op jit(solution)/shard_map/ppermute | solution.py:23
  125.4 4.0 %collective-permute-start = (bf16[128,4,64]{0,2,1:T(8,128)(2,1)S(1)}, bf16[128,4,64]{0,2,1:T(8,128)(2,1)S(1)}, u32[]{:S(2)}, u32[]{:S(2)}) collective-permute-start(bf16[128,4,64]{0,2,1:T(8,128)(2,1)S(1)} %bitcast.121), channel_id=1, source_target_pairs={{0,4},{4,8},{8,12},{12,16},{16,20},{20,24},{24,28},{28,32},{32,36}... | collective-permute-start | bytes 196616 | tf_op jit(solution)/shard_map/ppermute | solution.py:23
  129.3 2.2 slice-start
  129.4 2.8 slice-start.1
  132.2 2.2 copy-start.2
  136.7 47.9 %all-to-all-start = ((bf16[64,8,1440]{2,1,0:T(8,128)(2,1)}), bf16[64,8,1440]{2,1,0:T(8,128)(2,1)}, u32[]{:S(2)}, u32[]{:S(2)}) async-start(bf16[64,8,1440]{2,1,0:T(8,128)(2,1)} %bitcast.25), calls=%async_computation | async-start | bytes 3145728 | tf_op jit(solution)/shard_map/all_to_all | solution.py:168
  184.6 45.4 %all-to-all-start.2 = ((bf16[64,8,1440]{2,1,0:T(8,128)(2,1)}), bf16[64,8,1440]{2,1,0:T(8,128)(2,1)S(1)}, u32[]{:S(2)}, u32[]{:S(2)}) async-start(bf16[64,8,1440]{2,1,0:T(8,128)(2,1)} %bitcast.31), calls=%async_computation.2 | async-start | bytes 3145728 | tf_op jit(solution)/shard_map/all_to_all | solution.py:168
  230.1 1.2 copy-start.1
  231.2 45.4 %all-to-all-start.1 = ((bf16[64,8,1440]{2,1,0:T(8,128)(2,1)}), bf16[64,8,1440]{2,1,0:T(8,128)(2,1)S(1)}, u32[]{:S(2)}, u32[]{:S(2)}) async-start(bf16[64,8,1440]{2,1,0:T(8,128)(2,1)} %bitcast.114), calls=%async_computation.1 | async-start | bytes 3145728 | tf_op jit(solution)/shard_map/all_to_all | solution.py:171
  251.8 31.4 %copy-start.4 = (s32[128,4]{0,1:T(4,128)S(1)}, s32[128,4]{0,1:T(4,128)}, u32[]{:S(2)}) copy-start(s32[128,4]{0,1:T(4,128)} %param.19) | copy-start | bytes 6148
  276.7 45.5 %all-to-all-start.3 = ((bf16[64,8,1440]{2,1,0:T(8,128)(2,1)}), bf16[64,8,1440]{2,1,0:T(8,128)(2,1)}, u32[]{:S(2)}, u32[]{:S(2)}) async-start(bf16[64,8,1440]{2,1,0:T(8,128)(2,1)} %bitcast.113), calls=%async_computation.3 | async-start | bytes 3145728 | tf_op jit(solution)/shard_map/all_to_all | solution.py:171
Sparse Core Ops, SparseCore 0:
  10.1 97.2 all-gather.2
